TPU v7x, 32 devices: a whole 2x2x4 slice. The times are simulated.
32 devices in a mesh: ctx: 8 (over z, x), fsdp: 4 (over y, core).
Axes of the slice: x: 2, y: 2, z: 4, core: 2. Of those that a mesh axis runs over, the one named last changes fastest.
Arguments:
- layer_input: bfloat16 [2, 4, 1024, 1024], P(None, 'fsdp', 'ctx'), may hold values from -6 to 6
- segments: int32 [2, 4, 1024], P(None, 'fsdp', 'ctx'), may hold values from 0 to 15, never falling along the last dimension, each value on 1 to 512 neighbouring positions
- cotangent: bfloat16 [2, 4, 1024, 1024], P(None, 'fsdp', 'ctx'), may hold values from -6 to 6
- query_weight: bfloat16 [1024, 1024], P('fsdp'), may hold values from -0.1875 to 0.1875
- key_weight: bfloat16 [1024, 1024], P('fsdp'), may hold values from -0.1875 to 0.1875
- value_weight: bfloat16 [1024, 1024], P('fsdp'), may hold values from -0.1875 to 0.1875
- output_weight: bfloat16 [1024, 1024], P('fsdp'), may hold values from -0.75 to 0.75
- expand_weight: bfloat16 [1024, 4096], P('fsdp'), may hold values from -0.1875 to 0.1875
- contract_weight: bfloat16 [4096, 1024], P('fsdp'), may hold values from -0.09375 to 0.09375
- query_bias: bfloat16 [1024], P('fsdp'), may hold values from -3 to 3
- value_bias: bfloat16 [1024], P('fsdp'), may hold values from -3 to 3
- output_bias: bfloat16 [1024], P('fsdp'), may hold values from -3 to 3
- first_gain: bfloat16 [1024], P('fsdp'), may hold values from 0.099609375 to 1.8984375
- first_shift: bfloat16 [1024], P('fsdp'), may hold values from -3 to 3
- expand_bias: bfloat16 [4096], P('fsdp'), may hold values from -3 to 3
- contract_bias: bfloat16 [1024], P('fsdp'), may hold values from -3 to 3
- second_gain: bfloat16 [1024], P('fsdp'), may hold values from 0.099609375 to 1.8984375
- second_shift: bfloat16 [1024], P('fsdp'), may hold values from -3 to 3
Outputs:
- layer_output: bfloat16 [2, 4, 1024, 1024], P(None, 'fsdp', 'ctx')
- input_grad: float32 [2, 4, 1024, 1024], P(None, 'fsdp', 'ctx')
- query_weight_grad: float32 [1024, 1024], P('fsdp')
- key_weight_grad: float32 [1024, 1024], P('fsdp')
- value_weight_grad: float32 [1024, 1024], P('fsdp')
- output_weight_grad: float32 [1024, 1024], P('fsdp')
- expand_weight_grad: float32 [1024, 4096], P('fsdp')
- contract_weight_grad: float32 [4096, 1024], P('fsdp')
- query_bias_grad: float32 [1024], P('fsdp')
- value_bias_grad: float32 [1024], P('fsdp')
- output_bias_grad: float32 [1024], P('fsdp')
- first_gain_grad: float32 [1024], P('fsdp')
- first_shift_grad: float32 [1024], P('fsdp')
- expand_bias_grad: float32 [4096], P('fsdp')
- contract_bias_grad: float32 [1024], P('fsdp')
- second_gain_grad: float32 [1024], P('fsdp')
- second_shift_grad: float32 [1024], P('fsdp')
Inputs may be any that keep to these rules, and one draw needn't show every extreme that they name: `segments`: in each sequence the ids never fall along the positions; each document holds 1 to 512 positions, and one holds exactly 512.
All inputs are finite; a program needn't handle non-finite values.
Results may differ from a plain program's by a relative error of at most 0.025.
Values may be sent and summed in bfloat16 or wider, within the bound.
A program may use at most 192 MiB of HBM per device.

v0:
```python
import jax
import jax.numpy as jnp
from jax import lax
from jax.sharding import PartitionSpec as P

HEADS = 16
HEAD_DIM = 64


def as_sent(x):
    return jax.tree.map(lambda a: a.astype(jnp.bfloat16) if a.dtype == jnp.float32 else a, x)


def plain_dot(left_side, right_side):
    return jnp.dot(left_side, right_side, preferred_element_type=jnp.float32)


def left_dot(left_side, right_side):
    return lax.dot_general(
        left_side, right_side, (((0,), (0,)), ((), ())), preferred_element_type=jnp.float32
    )


def right_dot(left_side, right_side):
    return lax.dot_general(
        left_side, right_side, (((1,), (1,)), ((), ())), preferred_element_type=jnp.float32
    )


def norm_forward(hidden, gain_row, offset_row):
    centre = hidden - jnp.mean(hidden, axis=-1, keepdims=True)
    inverse = lax.rsqrt(jnp.mean(centre * centre, axis=-1, keepdims=True) + 1e-05)
    normed = centre * inverse
    return (normed * gain_row.astype(jnp.float32) + offset_row.astype(jnp.float32), normed, inverse)


def norm_backward(grad_out, normed, inverse, gain_row):
    scaled = grad_out * gain_row.astype(jnp.float32)
    grad_in = inverse * (
        scaled
        - jnp.mean(scaled, axis=-1, keepdims=True)
        - normed * jnp.mean(scaled * normed, axis=-1, keepdims=True)
    )
    return (grad_in, jnp.sum(grad_out * normed, axis=0), jnp.sum(grad_out, axis=0))


def gather_weights(shards):
    return (
        lax.all_gather(shards[0], "fsdp", axis=0, tiled=True),
        lax.all_gather(shards[1], "fsdp", axis=0, tiled=True),
        lax.all_gather(shards[2], "fsdp", axis=0, tiled=True),
        lax.all_gather(shards[3], "fsdp", axis=0, tiled=True),
        lax.all_gather(shards[4], "fsdp", axis=0, tiled=True),
        lax.all_gather(shards[5], "fsdp", axis=0, tiled=True),
        lax.all_gather(shards[6], "fsdp", axis=0, tiled=True),
        lax.all_gather(shards[7], "fsdp", axis=0, tiled=True),
        lax.all_gather(shards[8], "fsdp", axis=0, tiled=True),
        lax.all_gather(shards[9], "fsdp", axis=0, tiled=True),
        lax.all_gather(shards[10], "fsdp", axis=0, tiled=True),
        lax.all_gather(shards[11], "fsdp", axis=0, tiled=True),
        lax.all_gather(shards[12], "fsdp", axis=0, tiled=True),
        lax.all_gather(shards[13], "fsdp", axis=0, tiled=True),
        lax.all_gather(shards[14], "fsdp", axis=0, tiled=True),
    )


def attend_forward(query_bf, key_bf, value_bf, seg_local):
    row_count = query_bf.shape[0]
    score_scale = HEAD_DIM ** (-0.5)
    query_heads = query_bf.reshape(row_count, HEADS, HEAD_DIM)
    run_max = jnp.full((HEADS, row_count), -1e30, jnp.float32)
    key_rows = lax.all_gather(key_bf, "ctx", axis=0, tiled=True)
    value_rows = lax.all_gather(value_bf, "ctx", axis=0, tiled=True)
    key_seg = lax.all_gather(seg_local, "ctx", axis=0, tiled=True)
    piece_rows = key_rows.shape[0]
    key_heads = key_rows.reshape(piece_rows, HEADS, HEAD_DIM)
    value_heads = value_rows.reshape(piece_rows, HEADS, HEAD_DIM)
    scores = (
        jnp.einsum("rhd,khd->hrk", query_heads, key_heads, preferred_element_type=jnp.float32)
        * score_scale
    )
    same_doc = seg_local[:, None] == key_seg[None, :]
    scores = jnp.where(same_doc[None], scores, -1e30)
    new_max = jnp.maximum(run_max, jnp.max(scores, axis=-1))
    numerators = jnp.exp(scores - new_max[..., None])
    run_sum = jnp.sum(numerators, axis=-1)
    accumulated = jnp.einsum(
        "hrk,khd->hrd",
        numerators.astype(jnp.bfloat16),
        value_heads,
        preferred_element_type=jnp.float32,
    )
    run_max, run_sum, accumulated = (new_max, run_sum, accumulated)
    context = jnp.transpose(accumulated / run_sum[..., None], (1, 0, 2)).reshape(
        row_count, HEADS * HEAD_DIM
    )
    return (context, run_max + jnp.log(run_sum))


def block_grads(
    query_heads, grad_heads, query_seg, log_sum, row_delta, key_heads, value_heads, key_seg
):
    score_scale = HEAD_DIM ** (-0.5)
    scores = (
        jnp.einsum("rhd,khd->hrk", query_heads, key_heads, preferred_element_type=jnp.float32)
        * score_scale
    )
    same_doc = query_seg[:, None] == key_seg[None, :]
    scores = jnp.where(same_doc[None], scores, -1e30)
    probs_full = jnp.exp(scores - log_sum[..., None])
    grad_probs = jnp.einsum(
        "rhd,khd->hrk", grad_heads, value_heads, preferred_element_type=jnp.float32
    )
    grad_scores = (probs_full * (grad_probs - row_delta[..., None])).astype(jnp.bfloat16)
    return (probs_full, grad_scores)


def attend_backward(query_bf, key_bf, value_bf, seg_local, context, log_sum, grad_context):
    row_count = query_bf.shape[0]
    score_scale = HEAD_DIM ** (-0.5)
    key_every, value_every, seg_every = (
        lax.all_gather(key_bf, "ctx", axis=0, tiled=True),
        lax.all_gather(value_bf, "ctx", axis=0, tiled=True),
        lax.all_gather(seg_local, "ctx", axis=0, tiled=True),
    )
    length = key_every.shape[0]
    block_len = min(512, length)
    query_heads = query_bf.reshape(row_count, HEADS, HEAD_DIM)
    grad_heads = grad_context.reshape(row_count, HEADS, HEAD_DIM)
    row_delta = jnp.sum(
        (grad_context.astype(jnp.float32) * context).reshape(row_count, HEADS, HEAD_DIM), axis=-1
    ).T

    def visit_block(grad_query, block_num):
        first_row = block_num * block_len
        key_heads = lax.dynamic_slice_in_dim(key_every, first_row, block_len, 0).reshape(
            block_len, HEADS, HEAD_DIM
        )
        value_heads = lax.dynamic_slice_in_dim(value_every, first_row, block_len, 0).reshape(
            block_len, HEADS, HEAD_DIM
        )
        key_seg = lax.dynamic_slice_in_dim(seg_every, first_row, block_len, 0)
        probs_full, grad_scores = block_grads(
            query_heads, grad_heads, seg_local, log_sum, row_delta, key_heads, value_heads, key_seg
        )
        grad_query = (
            grad_query
            + jnp.einsum("hrk,khd->rhd", grad_scores, key_heads, preferred_element_type=jnp.float32)
            * score_scale
        )
        grad_keys = (
            jnp.einsum("hrk,rhd->khd", grad_scores, query_heads, preferred_element_type=jnp.float32)
            * score_scale
        )
        grad_values = jnp.einsum(
            "hrk,rhd->khd",
            probs_full.astype(jnp.bfloat16),
            grad_heads,
            preferred_element_type=jnp.float32,
        )
        stacked = jnp.stack(
            (
                grad_keys.reshape(block_len, HEADS * HEAD_DIM),
                grad_values.reshape(block_len, HEADS * HEAD_DIM),
            ),
            axis=1,
        )
        return (grad_query, stacked)

    grad_query, pieces = lax.scan(
        visit_block,
        jnp.zeros((row_count, HEADS, HEAD_DIM), jnp.float32),
        jnp.arange(length // block_len),
    )
    key_terms = pieces.reshape(length, 2, HEADS * HEAD_DIM)
    own_rows = lax.psum_scatter(
        key_terms.astype(jnp.bfloat16), "ctx", scatter_dimension=0, tiled=True
    ).astype(jnp.float32)
    grad_keyed = own_rows[:, 0].astype(jnp.bfloat16)
    grad_valued = own_rows[:, 1].astype(jnp.bfloat16)
    grad_queries = grad_query.reshape(row_count, HEADS * HEAD_DIM).astype(jnp.bfloat16)
    return (grad_queries, grad_keyed, grad_valued)


def layer_forward(inputs, seg_local, full_weights):
    (
        query_weight,
        key_weight,
        value_weight,
        output_weight,
        expand_weight,
        contract_weight,
        query_bias,
        value_bias,
        output_bias,
        first_gain,
        first_shift,
        expand_bias,
        contract_bias,
        second_gain,
        second_shift,
    ) = full_weights
    query_bf = (plain_dot(inputs, query_weight) + query_bias.astype(jnp.float32)).astype(
        jnp.bfloat16
    )
    key_bf = plain_dot(inputs, key_weight).astype(jnp.bfloat16)
    value_bf = (plain_dot(inputs, value_weight) + value_bias.astype(jnp.float32)).astype(
        jnp.bfloat16
    )
    context, log_sum = attend_forward(query_bf, key_bf, value_bf, seg_local)
    context_bf = context.astype(jnp.bfloat16)
    first_sum = (
        inputs.astype(jnp.float32)
        + plain_dot(context_bf, output_weight)
        + output_bias.astype(jnp.float32)
    )
    first_out, normed_one, inverse_one = norm_forward(first_sum, first_gain, first_shift)
    first_bf = first_out.astype(jnp.bfloat16)
    hidden = plain_dot(first_bf, expand_weight) + expand_bias.astype(jnp.float32)
    gelled_bf = jax.nn.gelu(hidden, approximate=False).astype(jnp.bfloat16)
    second_sum = (
        first_out + plain_dot(gelled_bf, contract_weight) + contract_bias.astype(jnp.float32)
    )
    result, normed_two, inverse_two = norm_forward(second_sum, second_gain, second_shift)
    kept_state = (
        query_bf,
        key_bf,
        value_bf,
        context,
        log_sum,
        context_bf,
        normed_one,
        inverse_one,
        first_bf,
        hidden,
        gelled_bf,
        normed_two,
        inverse_two,
    )
    return (result.astype(jnp.bfloat16), kept_state)


def layer_backward(inputs, seg_local, grad_out, kept_state, full_weights):
    (
        query_weight,
        key_weight,
        value_weight,
        output_weight,
        expand_weight,
        contract_weight,
        query_bias,
        value_bias,
        output_bias,
        first_gain,
        first_shift,
        expand_bias,
        contract_bias,
        second_gain,
        second_shift,
    ) = full_weights
    (
        query_bf,
        key_bf,
        value_bf,
        context,
        log_sum,
        context_bf,
        normed_one,
        inverse_one,
        first_bf,
        hidden,
        gelled_bf,
        normed_two,
        inverse_two,
    ) = kept_state
    grad_second, second_gain_grad, second_shift_grad = norm_backward(
        grad_out.astype(jnp.float32), normed_two, inverse_two, second_gain
    )
    grad_branch = grad_second.astype(jnp.bfloat16)
    contract_weight_grad = left_dot(gelled_bf, grad_branch)
    contract_bias_grad = jnp.sum(grad_branch.astype(jnp.float32), axis=0)
    grad_gelled = right_dot(grad_branch, contract_weight)
    gelu_pull = jax.vjp(lambda values: jax.nn.gelu(values, approximate=False), hidden)[1]
    grad_hidden = gelu_pull(grad_gelled)[0].astype(jnp.bfloat16)
    expand_weight_grad = left_dot(first_bf, grad_hidden)
    expand_bias_grad = jnp.sum(grad_hidden.astype(jnp.float32), axis=0)
    grad_first = grad_second + right_dot(grad_hidden, expand_weight)
    grad_attn, first_gain_grad, first_shift_grad = norm_backward(
        grad_first, normed_one, inverse_one, first_gain
    )
    grad_attn_low = grad_attn.astype(jnp.bfloat16)
    output_weight_grad = left_dot(context_bf, grad_attn_low)
    output_bias_grad = jnp.sum(grad_attn_low.astype(jnp.float32), axis=0)
    grad_context = right_dot(grad_attn_low, output_weight).astype(jnp.bfloat16)
    grad_queries, grad_keyed, grad_valued = attend_backward(
        query_bf, key_bf, value_bf, seg_local, context, log_sum, grad_context
    )
    query_weight_grad = left_dot(inputs, grad_queries)
    key_weight_grad = left_dot(inputs, grad_keyed)
    value_weight_grad = left_dot(inputs, grad_valued)
    query_bias_grad = jnp.sum(grad_queries.astype(jnp.float32), axis=0)
    value_bias_grad = jnp.sum(grad_valued.astype(jnp.float32), axis=0)
    grad_input = (
        grad_attn
        + right_dot(grad_queries, query_weight)
        + right_dot(grad_keyed, key_weight)
        + right_dot(grad_valued, value_weight)
    )
    grad_terms = (
        query_weight_grad,
        key_weight_grad,
        value_weight_grad,
        output_weight_grad,
        expand_weight_grad,
        contract_weight_grad,
        query_bias_grad,
        value_bias_grad,
        output_bias_grad,
        first_gain_grad,
        first_shift_grad,
        expand_bias_grad,
        contract_bias_grad,
        second_gain_grad,
        second_shift_grad,
    )
    return (grad_input, grad_terms)


def per_device(
    layer_input,
    segments,
    cotangent,
    query_weight,
    key_weight,
    value_weight,
    output_weight,
    expand_weight,
    contract_weight,
    query_bias,
    value_bias,
    output_bias,
    first_gain,
    first_shift,
    expand_bias,
    contract_bias,
    second_gain,
    second_shift,
):
    shards = (
        query_weight,
        key_weight,
        value_weight,
        output_weight,
        expand_weight,
        contract_weight,
        query_bias,
        value_bias,
        output_bias,
        first_gain,
        first_shift,
        expand_bias,
        contract_bias,
        second_gain,
        second_shift,
    )
    micro_count = layer_input.shape[0]
    results = []
    grad_inputs = []
    totals = None
    for micro_step in range(micro_count):
        inputs = layer_input[micro_step, 0]
        seg_local = segments[micro_step, 0].astype(jnp.bfloat16)
        front_weights = gather_weights(shards)
        result, kept_state = layer_forward(inputs, seg_local, front_weights)
        behind = gather_weights(shards)
        grad_input, grad_terms = layer_backward(
            inputs, seg_local, cotangent[micro_step, 0], kept_state, behind
        )
        results.append(result)
        grad_inputs.append(grad_input)
        if totals is None:
            totals = grad_terms
        else:
            totals = tuple(
                (left_side + right_side for left_side, right_side in zip(totals, grad_terms))
            )
    reduced = jax.tree.map(
        lambda part: part.astype(jnp.float32),
        lax.psum_scatter(as_sent(totals), "fsdp", scatter_dimension=0, tiled=True),
    )
    summed = jax.tree.map(lambda part: part.astype(jnp.float32), lax.psum(as_sent(reduced), "ctx"))
    layer_output = jnp.stack(results, axis=0)[:, None]
    input_grad = jnp.stack(grad_inputs, axis=0)[:, None]
    return (
        layer_output,
        input_grad,
        summed[0],
        summed[1],
        summed[2],
        summed[3],
        summed[4],
        summed[5],
        summed[6],
        summed[7],
        summed[8],
        summed[9],
        summed[10],
        summed[11],
        summed[12],
        summed[13],
        summed[14],
    )


def solution(mesh):
    in_specs = (
        P(None, "fsdp", "ctx", None),
        P(None, "fsdp", "ctx"),
        P(None, "fsdp", "ctx", None),
        P("fsdp", None),
        P("fsdp", None),
        P("fsdp", None),
        P("fsdp", None),
        P("fsdp", None),
        P("fsdp", None),
        P("fsdp"),
        P("fsdp"),
        P("fsdp"),
        P("fsdp"),
        P("fsdp"),
        P("fsdp"),
        P("fsdp"),
        P("fsdp"),
        P("fsdp"),
    )
    out_specs = (
        P(None, "fsdp", "ctx", None),
        P(None, "fsdp", "ctx", None),
        P("fsdp", None),
        P("fsdp", None),
        P("fsdp", None),
        P("fsdp", None),
        P("fsdp", None),
        P("fsdp", None),
        P("fsdp"),
        P("fsdp"),
        P("fsdp"),
        P("fsdp"),
        P("fsdp"),
        P("fsdp"),
        P("fsdp"),
        P("fsdp"),
        P("fsdp"),
    )
    return jax.shard_map(
        per_device, mesh=mesh, in_specs=in_specs, out_specs=out_specs, check_vma=False
    )
```

profile of v0, /device:TPU:0, one launch (start us, length us, event | category | flops | bytes accessed | tf_op | source)
XLA Modules:
  0.0 1220.2 jit_solution(14195021096110765214)
XLA Ops:
  16.1 18.8 %all-gather.27.cloned.1.call-done = bf16[1024,1024]{1,0:T(8,128)(2,1)} async-done(((bf16[256,1024]{1,0:T(8,128)(2,1)}), bf16[1024,1024]{1,0:T(8,128)(2,1)}) %all-gather.27.cloned.1.call-update) | async-done | bytes 2097168 | tf_op jit(solution)/shard_map/all_gather | solution.py:51
  37.8 21.3 %all-gather.23.cloned.1.call-done = bf16[1024,1024]{1,0:T(8,128)(2,1)} async-done(((bf16[256,1024]{1,0:T(8,128)(2,1)}), bf16[1024,1024]{1,0:T(8,128)(2,1)}) %all-gather.23.cloned.1.call-update) | async-done | bytes 2097168 | tf_op jit(solution)/shard_map/all_gather | solution.py:50
  103.9 20.6 %all-gather = bf16[1,1,1024]{2,1,0:T(2,128)(2,1)S(1)} all-gather(bf16[1,1,128]{2,1,0:T(2,128)(2,1)S(1)} %get-tuple-element.466), channel_id=2, replica_groups=mesh['ctx'=8,'fsdp'=4] {'ctx'}, dimensions={2}, use_global_device_ids=true | all-gather | bytes 2304 | tf_op jit(solution)/shard_map/all_gather | solution.py:74
  124.6 16.3 %all-gather.1 = bf16[1,1,1024]{2,1,0:T(2,128)(2,1)S(1)} all-gather(bf16[1,1,128]{2,1,0:T(2,128)(2,1)S(1)} %get-tuple-element.465), channel_id=3, replica_groups=mesh['ctx'=8,'fsdp'=4] {'ctx'}, dimensions={2}, use_global_device_ids=true | all-gather | bytes 2304 | tf_op jit(solution)/shard_map/all_gather | solution.py:74
  154.3 31.3 %all-gather.25.cloned.1.call-done = bf16[1024,1024]{1,0:T(8,128)(2,1)} async-done(((bf16[128,1024]{1,0:T(8,128)(2,1)}), bf16[1024,1024]{1,0:T(8,128)(2,1)}) %all-gather.25.cloned.1.call-update) | async-done | bytes 2097168 | tf_op jit(solution)/shard_map/all_gather | solution.py:72
  199.6 36.4 %all-gather.39.cloned.1.call-done = bf16[1024,1024]{1,0:T(8,128)(2,1)} async-done(((bf16[128,1024]{1,0:T(8,128)(2,1)}), bf16[1024,1024]{1,0:T(8,128)(2,1)}) %all-gather.39.cloned.1.call-update) | async-done | bytes 2097168 | tf_op jit(solution)/shard_map/all_gather | solution.py:73
  239.9 46.6 %all-gather.37.cloned.1.call-done = bf16[1024,1024]{1,0:T(8,128)(2,1)} async-done(((bf16[128,1024]{1,0:T(8,128)(2,1)}), bf16[1024,1024]{1,0:T(8,128)(2,1)}) %all-gather.37.cloned.1.call-update) | async-done | bytes 2097168 | tf_op jit(solution)/shard_map/all_gather | solution.py:72
  290.4 18.7 %all-gather.31.cloned.1.call-done = bf16[1024,1024]{1,0:T(8,128)(2,1)} async-done(((bf16[256,1024]{1,0:T(8,128)(2,1)}), bf16[1024,1024]{1,0:T(8,128)(2,1)}) %all-gather.31.cloned.1.call-update) | async-done | bytes 2097168 | tf_op jit(solution)/shard_map/all_gather | solution.py:52
  323.0 46.0 %all-gather.33.cloned.1.call-done = bf16[1024,4096]{1,0:T(8,128)(2,1)} async-done(((bf16[256,4096]{1,0:T(8,128)(2,1)}), bf16[1024,4096]{1,0:T(8,128)(2,1)}) %all-gather.33.cloned.1.call-update) | async-done | bytes 8388624 | tf_op jit(solution)/shard_map/all_gather | solution.py:53
  375.2 53.7 %all-gather.35.cloned.1.call-done = bf16[4096,1024]{1,0:T(8,128)(2,1)} async-done(((bf16[1024,1024]{1,0:T(8,128)(2,1)}), bf16[4096,1024]{1,0:T(8,128)(2,1)}) %all-gather.35.cloned.1.call-update) | async-done | bytes 8388624 | tf_op jit(solution)/shard_map/all_gather | solution.py:54
  479.9 34.4 %while.26 = (s32[]{:T(128)}, f32[128,16,64]{0,2,1:T(8,128)}, bf16[2,512,2,1024]{3,1,0,2:T(8,128)(2,1)}, s32[2]{0:T(128)S(1)}, bf16[1024,1024]{0,1:T(8,128)(2,1)}...) while((s32[]{:T(128)}, f32[128,16,64]{0,2,1:T(8,128)}, ...), condition=%wide.region_18.19_spmd.clone, body=%wide.region_17.18_spmd.clone.sunk | while | flops 684130304 | bytes 77819448 | solution.py:170
  523.5 34.9 %while.27 = (s32[]{:T(128)}, f32[128,16,64]{0,2,1:T(8,128)}, bf16[2,512,2,1024]{3,1,0,2:T(8,128)(2,1)}, s32[2]{0:T(128)S(1)}, bf16[1024,1024]{0,1:T(8,128)(2,1)}...) while((s32[]{:T(128)}, f32[128,16,64]{0,2,1:T(8,128)}, ...), condition=%wide.region_26.27_spmd.clone, body=%wide.region_25.26_spmd.clone.sunk | while | flops 684130304 | bytes 77819448 | solution.py:170
  566.6 35.8 %reduce-scatter.9.cloned.1.call-done = bf16[128,2,1024]{2,0,1:T(8,128)(2,1)} async-done(((bf16[1024,2,1024]{2,0,1:T(8,128)(2,1)}), bf16[128,2,1024]{2,0,1:T(8,128)(2,1)}) %reduce-scatter.9.cloned.1.call-update) | async-done | bytes 524304 | tf_op jit(solution)/shard_map/reduce_scatter | solution.py:176
  606.1 88.5 %reduce-scatter.11.cloned.1.call-done = bf16[128,2,1024]{2,0,1:T(8,128)(2,1)} async-done(((bf16[1024,2,1024]{2,0,1:T(8,128)(2,1)}), bf16[128,2,1024]{2,0,1:T(8,128)(2,1)}) %reduce-scatter.11.cloned.1.call-update) | async-done | bytes 524304 | tf_op jit(solution)/shard_map/reduce_scatter | solution.py:176
  712.5 11.8 add_convert_fusion.1
  736.8 12.7 %add_convert_fusion = bf16[4096,1024]{1,0:T(8,128)(2,1)} fusion(f32[4096,1024]{1,0:T(8,128)} %fusion.148, f32[128,1024]{1,0:T(8,128)S(1)} %copy-done.51, f32[128,4096]{1,0:T(8,128)S(1)} %copy-done.46), kind=kOutput, calls=%fused_computation.44 | convolution fusion | flops 1116340224 | bytes 27787264 | tf_op jit(solution)/shard_map/dot_general | solution.py:19
  749.9 12.6 %reduce-scatter.19.cloned.1.call-done = bf16[256,1024]{1,0:T(8,128)(2,1)} async-done(((bf16[1024,1024]{1,0:T(8,128)(2,1)}), bf16[256,1024]{1,0:T(8,128)(2,1)}) %reduce-scatter.19.cloned.1.call-update) | async-done | bytes 524304 | tf_op jit(solution)/shard_map/reduce_scatter | solution.py:389
  762.4 34.4 %reduce-scatter.15.cloned.1.call-done = bf16[256,1024]{0,1:T(8,128)(2,1)} async-done(((bf16[1024,1024]{0,1:T(8,128)(2,1)}), bf16[256,1024]{0,1:T(8,128)(2,1)}) %reduce-scatter.15.cloned.1.call-update) | async-done | bytes 524304 | tf_op jit(solution)/shard_map/reduce_scatter | solution.py:389
  796.8 34.6 %reduce-scatter.17.cloned.1.call-done = bf16[256,1024]{0,1:T(8,128)(2,1)} async-done(((bf16[1024,1024]{0,1:T(8,128)(2,1)}), bf16[256,1024]{0,1:T(8,128)(2,1)}) %reduce-scatter.17.cloned.1.call-update) | async-done | bytes 524304 | tf_op jit(solution)/shard_map/reduce_scatter | solution.py:389
  831.4 74.2 %reduce-scatter.21.cloned.1.call-done = bf16[256,4096]{1,0:T(8,128)(2,1)} async-done(((bf16[1024,4096]{1,0:T(8,128)(2,1)}), bf16[256,4096]{1,0:T(8,128)(2,1)}) %reduce-scatter.21.cloned.1.call-update) | async-done | bytes 2097168 | tf_op jit(solution)/shard_map/reduce_scatter | solution.py:389
  905.6 74.4 %reduce-scatter.23.cloned.1.call-done = bf16[1024,1024]{1,0:T(8,128)(2,1)} async-done(((bf16[4096,1024]{1,0:T(8,128)(2,1)}), bf16[1024,1024]{1,0:T(8,128)(2,1)}) %reduce-scatter.23.cloned.1.call-update) | async-done | bytes 2097168 | tf_op jit(solution)/shard_map/reduce_scatter | solution.py:389
  990.1 11.3 all-reduce.11
  1002.0 23.1 %all-reduce.9 = (bf16[256]{0:T(256)(128)(2,1)S(1)}, bf16[256]{0:T(256)(128)(2,1)S(1)}, bf16[256]{0:T(256)(128)(2,1)S(1)}, bf16[256]{0:T(256)(128)(2,1)S(1)}, bf1...) all-reduce(bf16[256]{0:T(256)(128)(2,1)S(1)} %dynamic-slice.1, ...), channel_id=1, replica_groups=mesh['ctx'=8,'fsdp'=4] {'ctx'}, use_global_device_ids=true, to_apply=%region_43.44 | all-reduce | flops 3072 | bytes 12288 | tf_op jit(solution)/shard_map/psum | solution.py:391
  1037.3 164.2 %all-reduce.14.cloned.1.call-done = (bf16[256,1024]{0,1:T(8,128)(2,1)}, bf16[256,1024]{0,1:T(8,128)(2,1)}, bf16[256,1024]{0,1:T(8,128)(2,1)}, bf16[256,1024]{1,0...) async-done(((bf16[256,1024]{0,1:T(8,128)(2,1)}, bf16[256,1024]{0,1:T(8,128)(2,1)}, bf16[256,1024]{0,1:T(8,128)(2,1)}, bf16[256,1024]{1,0:T(8,128)(2,1)}, ...) | async-done | bytes 6291472 | tf_op jit(solution)/shard_map/psum | solution.py:391
  (464 shorter events, 312.7 us)
Async XLA Ops:
  7.2 27.7 %all-gather.27.cloned.1.call-start = ((), (), s32[]{:S(2)}) async-start(), calls=%async_computation.11 | async-start | bytes 2621440 | tf_op jit(solution)/shard_map/all_gather | solution.py:51
  7.9 51.2 %all-gather.23.cloned.1.call-start = ((), (), s32[]{:S(2)}) async-start(), calls=%async_computation.9 | async-start | bytes 2621440 | tf_op jit(solution)/shard_map/all_gather | solution.py:50
  8.7 138.5 %all-gather.21.cloned.1.call-start = ((), (), s32[]{:S(2)}) async-start(), calls=%async_computation.8 | async-start | bytes 2621440 | tf_op jit(solution)/shard_map/all_gather | solution.py:49
  9.4 140.9 %all-gather.29.cloned.1.call-start = ((), (), s32[]{:S(2)}) async-start(), calls=%async_computation.12 | async-start | bytes 2359296 | tf_op jit(solution)/shard_map/all_gather | solution.py:73
  37.8 147.9 %all-gather.25.cloned.1.call-start = ((), (), s32[]{:S(2)}) async-start(), calls=%async_computation.10 | async-start | bytes 2359296 | tf_op jit(solution)/shard_map/all_gather | solution.py:72
  61.9 174.1 %all-gather.39.cloned.1.call-start = ((), (), s32[]{:S(2)}) async-start(), calls=%async_computation.17 | async-start | bytes 2359296 | tf_op jit(solution)/shard_map/all_gather | solution.py:73
  63.1 223.4 %all-gather.37.cloned.1.call-start = ((), (), s32[]{:S(2)}) async-start(), calls=%async_computation.16 | async-start | bytes 2359296 | tf_op jit(solution)/shard_map/all_gather | solution.py:72
  65.9 243.3 %all-gather.31.cloned.1.call-start = ((), (), s32[]{:S(2)}) async-start(), calls=%async_computation.13 | async-start | bytes 2621440 | tf_op jit(solution)/shard_map/all_gather | solution.py:52
  66.8 302.3 %all-gather.33.cloned.1.call-start = ((), (), s32[]{:S(2)}) async-start(), calls=%async_computation.14 | async-start | bytes 10485760 | tf_op jit(solution)/shard_map/all_gather | solution.py:53
  67.5 361.4 %all-gather.35.cloned.1.call-start = ((), (), s32[]{:S(2)}) async-start(), calls=%async_computation.15 | async-start | bytes 10485760 | tf_op jit(solution)/shard_map/all_gather | solution.py:54
  68.1 534.3 %reduce-scatter.9.cloned.1.call-start = ((), (), s32[]{:S(2)}) async-start(), calls=%async_computation.18 | async-start | bytes 4718592 | tf_op jit(solution)/shard_map/reduce_scatter | solution.py:176
  93.7 346.5 %copy-start.56 = (f32[4,1,256]{2,1,0:T(1,128)}, f32[4,1,256]{2,1,0:T(1,128)S(1)}, u32[]{:S(2)}) copy-start(f32[4,1,256]{2,1,0:T(1,128)S(1)} %convert_element_type.499) | copy-start | bytes 12292
  150.2 161.3 %copy-start.4 = (bf16[128,1024]{0,1:T(8,128)(2,1)}, bf16[128,1024]{0,1:T(8,128)(2,1)S(1)}, u32[]{:S(2)}) copy-start(bf16[128,1024]{0,1:T(8,128)(2,1)S(1)} %copy.100) | copy-start | bytes 786436
  311.3 159.6 %copy-start.15 = (f32[128,1024]{1,0:T(8,128)}, f32[128,1024]{1,0:T(8,128)S(1)}, u32[]{:S(2)}) copy-start(f32[128,1024]{1,0:T(8,128)S(1)} %get-tuple-element.470) | copy-start | bytes 1572868
  311.3 159.6 %copy-start.74 = (f32[128]{0:T(128)}, f32[128]{0:T(128)S(1)}, u32[]{:S(2)}) copy-start(f32[128]{0:T(128)S(1)} %broadcast_multiply_fusion.11) | copy-start | bytes 1540
  323.0 148.0 %copy-start.76 = (f32[128]{0:T(128)}, f32[128]{0:T(128)S(1)}, u32[]{:S(2)}) copy-start(f32[128]{0:T(128)S(1)} %add_rsqrt_fusion.3) | copy-start | bytes 1540
  514.4 180.3 %reduce-scatter.11.cloned.1.call-start = ((), (), s32[]{:S(2)}) async-start(), calls=%async_computation.19 | async-start | bytes 4718592 | tf_op jit(solution)/shard_map/reduce_scatter | solution.py:176
  558.4 191.5 %reduce-scatter.13.cloned.1.call-start = ((), (), s32[]{:S(2)}) async-start(), calls=%async_computation.20 | async-start | bytes 2621440 | tf_op jit(solution)/shard_map/reduce_scatter | solution.py:389
  562.7 199.7 %reduce-scatter.19.cloned.1.call-start = ((), (), s32[]{:S(2)}) async-start(), calls=%async_computation.23 | async-start | bytes 2621440 | tf_op jit(solution)/shard_map/reduce_scatter | solution.py:389
  566.6 230.2 %reduce-scatter.15.cloned.1.call-start = ((), (), s32[]{:S(2)}) async-start(), calls=%async_computation.21 | async-start | bytes 2621440 | tf_op jit(solution)/shard_map/reduce_scatter | solution.py:389
  699.0 132.4 %reduce-scatter.17.cloned.1.call-start = ((), (), s32[]{:S(2)}) async-start(), calls=%async_computation.22 | async-start | bytes 2621440 | tf_op jit(solution)/shard_map/reduce_scatter | solution.py:389
  702.9 202.7 %reduce-scatter.21.cloned.1.call-start = ((), (), s32[]{:S(2)}) async-start(), calls=%async_computation.24 | async-start | bytes 10485760 | tf_op jit(solution)/shard_map/reduce_scatter | solution.py:389
  724.3 255.6 %reduce-scatter.23.cloned.1.call-start = ((), (), s32[]{:S(2)}) async-start(), calls=%async_computation.25 | async-start | bytes 10485760 | tf_op jit(solution)/shard_map/reduce_scatter | solution.py:389
  749.6 451.9 %all-reduce.14.cloned.1.call-start = ((), (), s32[]{:S(2)}) async-start(), calls=%async_computation.26 | async-start | bytes 12582912 | tf_op jit(solution)/shard_map/psum | solution.py:391
  (103 other events, 952.1 us)
Sparse Core Ops, SparseCore 0:
  9.6 25.2 all-gather.26
  36.5 22.5 all-gather.22
  60.7 22.6 all-gather.20
  85.9 49.3 all-gather.28
  137.8 47.7 all-gather.24
  188.2 47.7 all-gather.38
  238.7 47.7 all-gather.36
  288.1 21.0 all-gather.30
  310.8 58.2 all-gather.32
  370.5 58.3 all-gather.34
  514.5 87.8 reduce-scatter.8
  606.9 87.6 reduce-scatter.10
  697.2 31.1 reduce-scatter.12
  730.9 31.4 reduce-scatter.18
  765.4 31.4 reduce-scatter.14
  799.9 31.3 reduce-scatter.16
  833.8 71.7 reduce-scatter.20
  908.2 71.6 reduce-scatter.22
  984.9 216.5 all-reduce.13
where the time goes:
time: 1230 us; the launch traced here: 1220 us
  waiting for transfers between devices  796 us (65%)
  matrix products  178 us (14%)
  blocking collectives  118 us (10%)
  local copies, waits for them, and re-layouts  74.1 us (6%)
  other arithmetic  32.8 us (3%)
  between operations  16.8 us (1%)
    reduce_scatter x6, waiting for transfers between devices, per_device(): lax.psum_scatter(as_sent(totals), 'fsdp', scatter_dimension=0, tiled=True)  230 us
    psum x1, waiting for transfers between devices, per_device(): lax.psum(as_sent(reduced), 'ctx')  164 us
    reduce_scatter x2, waiting for transfers between devices, attend_backward(): lax.psum_scatter(key_terms.astype(jnp.bfloat16), 'ctx', scatter_dimension...  124 us
    all_gather x2, waiting for transfers between devices, attend_forward(): key_rows = lax.all_gather(key_bf, 'ctx', axis=0, tiled=True)  77.9 us
    dot_general x12, matrix products, left_dot(): lax.dot_general(left_side, right_side, (((0,), (0,)), ((), ())), preferre...  60 us
    all_gather x1, waiting for transfers between devices, gather_weights(): lax.all_gather(shards[5], 'fsdp', axis=0, tiled=True)  53.7 us
    all_gather x1, waiting for transfers between devices, gather_weights(): lax.all_gather(shards[4], 'fsdp', axis=0, tiled=True)  46 us
    dot_general x12, matrix products, plain_dot(): return jnp.dot(left_side, right_side, preferred_element_type=jnp.float32)  37.6 us
  transfers between devices with their start and end apart: 19, of which 16 were waited for; matrix products, arithmetic and copies ran while one was open for 15% of the time, Pallas kernels for 0%

commit v1 on v0

--- a/solution.py
+++ b/solution.py
@@ -71,7 +71,19 @@
     run_max = jnp.full((HEADS, row_count), -1e30, jnp.float32)
     key_rows = lax.all_gather(key_bf, "ctx", axis=0, tiled=True)
     value_rows = lax.all_gather(value_bf, "ctx", axis=0, tiled=True)
-    key_seg = lax.all_gather(seg_local, "ctx", axis=0, tiled=True)
+    axis_total = lax.axis_size("ctx")
+    buffers = [seg_local]
+    for p in range(axis_total - 1):
+        buffers.append(
+            lax.ppermute(
+                buffers[-1], "ctx", [(k0, (k0 + 1) % axis_total) for k0 in range(axis_total)]
+            )
+        )
+    key_seg = jnp.roll(
+        jnp.concatenate(buffers[::-1], axis=0),
+        shift=(lax.axis_index("ctx") + 1) * seg_local.shape[0],
+        axis=0,
+    )
     piece_rows = key_rows.shape[0]
     key_heads = key_rows.reshape(piece_rows, HEADS, HEAD_DIM)
     value_heads = value_rows.reshape(piece_rows, HEADS, HEAD_DIM)

time: 1230 us -> 1230 us (level)
    ppermute x0 -> x14, waiting for transfers between devices: none -> 36.6 us  [attend_forward(): lax.ppermute(buffers[-1], 'ctx', [(k0, (k0 + 1) % axis_total) for k0 in r...]
    all_gather x2, waiting for transfers between devices: 77.9 us -> 51 us  [attend_forward(): key_rows = lax.all_gather(key_bf, 'ctx', axis=0, tiled=True)]
    reduce_scatter x2, waiting for transfers between devices: 124 us -> 104 us  [attend_backward(): lax.psum_scatter(key_terms.astype(jnp.bfloat16), 'ctx', scatter_dimension...]
  transfers between devices with their start and end apart: 19 -> 33, of which waited for: 16 -> 27; matrix products, arithmetic and copies ran while one was open for 15% -> 15% of each run, Pallas kernels for 0% -> 0%
where the time goes in v1:
time: 1230 us; the launch traced here: 1220 us
  waiting for transfers between devices  786 us (64%)
  matrix products  178 us (14%)
  blocking collectives  121 us (10%)
  local copies, waits for them, and re-layouts  77.1 us (6%)
  other arithmetic  33 us (3%)
  between operations  16.9 us (1%)
    reduce_scatter x6, waiting for transfers between devices, per_device(): lax.psum_scatter(as_sent(totals), 'fsdp', scatter_dimension=0, tiled=True)  230 us
    psum x1, waiting for transfers between devices, per_device(): lax.psum(as_sent(reduced), 'ctx')  164 us
    reduce_scatter x2, waiting for transfers between devices, attend_backward(): lax.psum_scatter(key_terms.astype(jnp.bfloat16), 'ctx', scatter_dimension...  104 us
    dot_general x12, matrix products, left_dot(): lax.dot_general(left_side, right_side, (((0,), (0,)), ((), ())), preferre...  60.1 us
    all_gather x1, waiting for transfers between devices, gather_weights(): lax.all_gather(shards[5], 'fsdp', axis=0, tiled=True)  53.8 us
    all_gather x2, waiting for transfers between devices, attend_forward(): key_rows = lax.all_gather(key_bf, 'ctx', axis=0, tiled=True)  51 us
    all_gather x1, waiting for transfers between devices, gather_weights(): lax.all_gather(shards[4], 'fsdp', axis=0, tiled=True)  46.6 us
    all_gather x2, blocking collectives, attend_backward(): lax.all_gather(seg_local, 'ctx', axis=0, tiled=True)  40.3 us
  transfers between devices with their start and end apart: 33, of which 27 were waited for; matrix products, arithmetic and copies ran while one was open for 15% of the time, Pallas kernels for 0%

profile of v1, /device:TPU:0, one launch (start us, length us, event | category | flops | bytes accessed | tf_op | source)
XLA Modules:
  0.0 1220.7 jit_solution(4448056189988579757)
XLA Ops:
  16.1 18.8 %all-gather.27.cloned.1.call-done = bf16[1024,1024]{1,0:T(8,128)(2,1)} async-done(((bf16[256,1024]{1,0:T(8,128)(2,1)}), bf16[1024,1024]{1,0:T(8,128)(2,1)}) %all-gather.27.cloned.1.call-update) | async-done | bytes 2097168 | tf_op jit(solution)/shard_map/all_gather | solution.py:51
  37.8 21.3 %all-gather.23.cloned.1.call-done = bf16[1024,1024]{1,0:T(8,128)(2,1)} async-done(((bf16[256,1024]{1,0:T(8,128)(2,1)}), bf16[1024,1024]{1,0:T(8,128)(2,1)}) %all-gather.23.cloned.1.call-update) | async-done | bytes 2097168 | tf_op jit(solution)/shard_map/all_gather | solution.py:50
  107.2 19.5 %all-gather = bf16[1,1,1024]{2,1,0:T(2,128)(2,1)S(1)} all-gather(bf16[1,1,128]{2,1,0:T(2,128)(2,1)S(1)} %get-tuple-element.464), channel_id=2, replica_groups=mesh['ctx'=8,'fsdp'=4] {'ctx'}, dimensions={2}, use_global_device_ids=true | all-gather | bytes 2304 | tf_op jit(solution)/shard_map/all_gather | solution.py:136
  199.0 37.0 %all-gather.39.cloned.1.call-done = bf16[1024,1024]{1,0:T(8,128)(2,1)} async-done(((bf16[128,1024]{1,0:T(8,128)(2,1)}), bf16[1024,1024]{1,0:T(8,128)(2,1)}) %all-gather.39.cloned.1.call-update) | async-done | bytes 2097168 | tf_op jit(solution)/shard_map/all_gather | solution.py:73
  239.9 46.6 %all-gather.37.cloned.1.call-done = bf16[1024,1024]{1,0:T(8,128)(2,1)} async-done(((bf16[128,1024]{1,0:T(8,128)(2,1)}), bf16[1024,1024]{1,0:T(8,128)(2,1)}) %all-gather.37.cloned.1.call-update) | async-done | bytes 2097168 | tf_op jit(solution)/shard_map/all_gather | solution.py:72
  290.6 18.6 %all-gather.31.cloned.1.call-done = bf16[1024,1024]{1,0:T(8,128)(2,1)} async-done(((bf16[256,1024]{1,0:T(8,128)(2,1)}), bf16[1024,1024]{1,0:T(8,128)(2,1)}) %all-gather.31.cloned.1.call-update) | async-done | bytes 2097168 | tf_op jit(solution)/shard_map/all_gather | solution.py:52
  322.5 46.6 %all-gather.33.cloned.1.call-done = bf16[1024,4096]{1,0:T(8,128)(2,1)} async-done(((bf16[256,4096]{1,0:T(8,128)(2,1)}), bf16[1024,4096]{1,0:T(8,128)(2,1)}) %all-gather.33.cloned.1.call-update) | async-done | bytes 8388624 | tf_op jit(solution)/shard_map/all_gather | solution.py:53
  375.1 53.8 %all-gather.35.cloned.1.call-done = bf16[4096,1024]{1,0:T(8,128)(2,1)} async-done(((bf16[1024,1024]{1,0:T(8,128)(2,1)}), bf16[4096,1024]{1,0:T(8,128)(2,1)}) %all-gather.35.cloned.1.call-update) | async-done | bytes 8388624 | tf_op jit(solution)/shard_map/all_gather | solution.py:54
  480.1 34.4 %while.26 = (s32[]{:T(128)}, f32[128,16,64]{0,2,1:T(8,128)}, bf16[2,512,2,1024]{3,1,0,2:T(8,128)(2,1)}, s32[2]{0:T(128)S(1)}, bf16[1024,1024]{0,1:T(8,128)(2,1)}...) while((s32[]{:T(128)}, f32[128,16,64]{0,2,1:T(8,128)}, ...), condition=%wide.region_18.20_spmd.clone, body=%wide.region_17.19_spmd.clone.sunk | while | flops 684130304 | bytes 77819448 | solution.py:182
  515.2 20.8 %all-gather.1 = bf16[1,1,1024]{2,1,0:T(2,128)(2,1)S(1)} all-gather(bf16[1,1,128]{2,1,0:T(2,128)(2,1)S(1)} %copy-done.86), channel_id=3, replica_groups=mesh['ctx'=8,'fsdp'=4] {'ctx'}, dimensions={2}, use_global_device_ids=true | all-gather | bytes 2304 | tf_op jit(solution)/shard_map/all_gather | solution.py:136
  544.1 34.6 %while.27 = (s32[]{:T(128)}, f32[128,16,64]{0,2,1:T(8,128)}, bf16[2,512,2,1024]{3,1,0,2:T(8,128)(2,1)}, s32[2]{0:T(128)S(1)}, bf16[1024,1024]{0,1:T(8,128)(2,1)}...) while((s32[]{:T(128)}, f32[128,16,64]{0,2,1:T(8,128)}, ...), condition=%wide.region_26.28_spmd.clone, body=%wide.region_25.27_spmd.clone.sunk | while | flops 684130304 | bytes 77819448 | solution.py:182
  587.1 15.8 %reduce-scatter.9.cloned.1.call-done = bf16[128,2,1024]{2,0,1:T(8,128)(2,1)} async-done(((bf16[1024,2,1024]{2,0,1:T(8,128)(2,1)}), bf16[128,2,1024]{2,0,1:T(8,128)(2,1)}) %reduce-scatter.9.cloned.1.call-update) | async-done | bytes 524304 | tf_op jit(solution)/shard_map/reduce_scatter | solution.py:188
  606.5 88.7 %reduce-scatter.11.cloned.1.call-done = bf16[128,2,1024]{2,0,1:T(8,128)(2,1)} async-done(((bf16[1024,2,1024]{2,0,1:T(8,128)(2,1)}), bf16[128,2,1024]{2,0,1:T(8,128)(2,1)}) %reduce-scatter.11.cloned.1.call-update) | async-done | bytes 524304 | tf_op jit(solution)/shard_map/reduce_scatter | solution.py:188
  713.1 11.9 add_convert_fusion.1
  726.5 10.9 fusion.150
  737.5 12.7 %add_convert_fusion = bf16[4096,1024]{1,0:T(8,128)(2,1)} fusion(f32[4096,1024]{1,0:T(8,128)} %fusion.150, f32[128,1024]{1,0:T(8,128)S(1)} %copy-done.51, f32[128,4096]{1,0:T(8,128)S(1)} %copy-done.46), kind=kOutput, calls=%fused_computation.44 | convolution fusion | flops 1116340224 | bytes 27787264 | tf_op jit(solution)/shard_map/dot_general | solution.py:19
  750.5 12.5 %reduce-scatter.19.cloned.1.call-done = bf16[256,1024]{1,0:T(8,128)(2,1)} async-done(((bf16[1024,1024]{1,0:T(8,128)(2,1)}), bf16[256,1024]{1,0:T(8,128)(2,1)}) %reduce-scatter.19.cloned.1.call-update) | async-done | bytes 524304 | tf_op jit(solution)/shard_map/reduce_scatter | solution.py:401
  763.0 34.4 %reduce-scatter.15.cloned.1.call-done = bf16[256,1024]{0,1:T(8,128)(2,1)} async-done(((bf16[1024,1024]{0,1:T(8,128)(2,1)}), bf16[256,1024]{0,1:T(8,128)(2,1)}) %reduce-scatter.15.cloned.1.call-update) | async-done | bytes 524304 | tf_op jit(solution)/shard_map/reduce_scatter | solution.py:401
  797.4 34.6 %reduce-scatter.17.cloned.1.call-done = bf16[256,1024]{0,1:T(8,128)(2,1)} async-done(((bf16[1024,1024]{0,1:T(8,128)(2,1)}), bf16[256,1024]{0,1:T(8,128)(2,1)}) %reduce-scatter.17.cloned.1.call-update) | async-done | bytes 524304 | tf_op jit(solution)/shard_map/reduce_scatter | solution.py:401
  831.9 74.2 %reduce-scatter.21.cloned.1.call-done = bf16[256,4096]{1,0:T(8,128)(2,1)} async-done(((bf16[1024,4096]{1,0:T(8,128)(2,1)}), bf16[256,4096]{1,0:T(8,128)(2,1)}) %reduce-scatter.21.cloned.1.call-update) | async-done | bytes 2097168 | tf_op jit(solution)/shard_map/reduce_scatter | solution.py:401
  906.2 74.4 %reduce-scatter.23.cloned.1.call-done = bf16[1024,1024]{1,0:T(8,128)(2,1)} async-done(((bf16[4096,1024]{1,0:T(8,128)(2,1)}), bf16[1024,1024]{1,0:T(8,128)(2,1)}) %reduce-scatter.23.cloned.1.call-update) | async-done | bytes 2097168 | tf_op jit(solution)/shard_map/reduce_scatter | solution.py:401
  990.7 11.3 all-reduce.11
  1002.6 23.1 %all-reduce.9 = (bf16[256]{0:T(256)(128)(2,1)S(1)}, bf16[256]{0:T(256)(128)(2,1)S(1)}, bf16[256]{0:T(256)(128)(2,1)S(1)}, bf16[256]{0:T(256)(128)(2,1)S(1)}, bf1...) all-reduce(bf16[256]{0:T(256)(128)(2,1)S(1)} %dynamic-slice.1, ...), channel_id=1, replica_groups=mesh['ctx'=8,'fsdp'=4] {'ctx'}, use_global_device_ids=true, to_apply=%region_43.45 | all-reduce | flops 3072 | bytes 12288 | tf_op jit(solution)/shard_map/psum | solution.py:403
  1037.9 164.1 %all-reduce.14.cloned.1.call-done = (bf16[256,1024]{0,1:T(8,128)(2,1)}, bf16[256,1024]{0,1:T(8,128)(2,1)}, bf16[256,1024]{0,1:T(8,128)(2,1)}, bf16[256,1024]{1,0...) async-done(((bf16[256,1024]{0,1:T(8,128)(2,1)}, bf16[256,1024]{0,1:T(8,128)(2,1)}, bf16[256,1024]{0,1:T(8,128)(2,1)}, bf16[256,1024]{1,0:T(8,128)(2,1)}, ...) | async-done | bytes 6291472 | tf_op jit(solution)/shard_map/psum | solution.py:403
  (506 shorter events, 349.3 us)
Async XLA Ops:
  7.2 27.7 %all-gather.27.cloned.1.call-start = ((), (), s32[]{:S(2)}) async-start(), calls=%async_computation.11 | async-start | bytes 2621440 | tf_op jit(solution)/shard_map/all_gather | solution.py:51
  7.9 51.2 %all-gather.23.cloned.1.call-start = ((), (), s32[]{:S(2)}) async-start(), calls=%async_computation.9 | async-start | bytes 2621440 | tf_op jit(solution)/shard_map/all_gather | solution.py:50
  8.7 164.8 %all-gather.21.cloned.1.call-start = ((), (), s32[]{:S(2)}) async-start(), calls=%async_computation.8 | async-start | bytes 2621440 | tf_op jit(solution)/shard_map/all_gather | solution.py:49
  9.4 167.1 %all-gather.29.cloned.1.call-start = ((), (), s32[]{:S(2)}) async-start(), calls=%async_computation.12 | async-start | bytes 2359296 | tf_op jit(solution)/shard_map/all_gather | solution.py:73
  37.8 147.3 %all-gather.25.cloned.1.call-start = ((), (), s32[]{:S(2)}) async-start(), calls=%async_computation.10 | async-start | bytes 2359296 | tf_op jit(solution)/shard_map/all_gather | solution.py:72
  61.9 174.1 %all-gather.39.cloned.1.call-start = ((), (), s32[]{:S(2)}) async-start(), calls=%async_computation.17 | async-start | bytes 2359296 | tf_op jit(solution)/shard_map/all_gather | solution.py:73
  63.1 223.4 %all-gather.37.cloned.1.call-start = ((), (), s32[]{:S(2)}) async-start(), calls=%async_computation.16 | async-start | bytes 2359296 | tf_op jit(solution)/shard_map/all_gather | solution.py:72
  65.9 243.3 %all-gather.31.cloned.1.call-start = ((), (), s32[]{:S(2)}) async-start(), calls=%async_computation.13 | async-start | bytes 2621440 | tf_op jit(solution)/shard_map/all_gather | solution.py:52
  66.8 302.3 %all-gather.33.cloned.1.call-start = ((), (), s32[]{:S(2)}) async-start(), calls=%async_computation.14 | async-start | bytes 10485760 | tf_op jit(solution)/shard_map/all_gather | solution.py:53
  67.5 361.4 %all-gather.35.cloned.1.call-start = ((), (), s32[]{:S(2)}) async-start(), calls=%async_computation.15 | async-start | bytes 10485760 | tf_op jit(solution)/shard_map/all_gather | solution.py:54
  68.1 534.8 %reduce-scatter.9.cloned.1.call-start = ((), (), s32[]{:S(2)}) async-start(), calls=%async_computation.18 | async-start | bytes 4718592 | tf_op jit(solution)/shard_map/reduce_scatter | solution.py:188
  68.7 63.2 %collective-permute-start = (bf16[128]{0:T(256)(128)(2,1)S(1)}, bf16[128]{0:T(256)(128)(2,1)S(1)}, u32[]{:S(2)}, u32[]{:S(2)}) collective-permute-start(bf16[128]{0:T(256)(128)(2,1)S(1)} %get-tuple-element.703), channel_id=1, source_target_pairs={{0,4},{4,8},{8,12},{12,16},{16,20},{20,24},{24,28},{28,0},{1,5},{5... | collective-permute-start | bytes 776 | tf_op jit(solution)/shard_map/ppermute | solution.py:78
  70.2 61.7 %collective-permute-start.7 = (bf16[128]{0:T(256)(128)(2,1)S(1)}, bf16[128]{0:T(256)(128)(2,1)S(1)}, u32[]{:S(2)}, u32[]{:S(2)}) collective-permute-start(bf16[128]{0:T(256)(128)(2,1)S(1)} %get-tuple-element.655), channel_id=1, source_target_pairs={{0,4},{4,8},{8,12},{12,16},{16,20},{20,24},{24,28},{28,0},{1,5},{5... | collective-permute-start | bytes 776 | tf_op jit(solution)/shard_map/ppermute | solution.py:78
  131.9 6.3 collective-permute-start.8
  163.0 6.3 collective-permute-start.6
  163.2 7.6 collective-permute-start.13
  514.6 180.7 %reduce-scatter.11.cloned.1.call-start = ((), (), s32[]{:S(2)}) async-start(), calls=%async_computation.19 | async-start | bytes 4718592 | tf_op jit(solution)/shard_map/reduce_scatter | solution.py:188
  578.8 171.7 %reduce-scatter.13.cloned.1.call-start = ((), (), s32[]{:S(2)}) async-start(), calls=%async_computation.20 | async-start | bytes 2621440 | tf_op jit(solution)/shard_map/reduce_scatter | solution.py:401
  583.1 179.9 %reduce-scatter.19.cloned.1.call-start = ((), (), s32[]{:S(2)}) async-start(), calls=%async_computation.23 | async-start | bytes 2621440 | tf_op jit(solution)/shard_map/reduce_scatter | solution.py:401
  587.0 210.4 %reduce-scatter.15.cloned.1.call-start = ((), (), s32[]{:S(2)}) async-start(), calls=%async_computation.21 | async-start | bytes 2621440 | tf_op jit(solution)/shard_map/reduce_scatter | solution.py:401
  699.6 132.3 %reduce-scatter.17.cloned.1.call-start = ((), (), s32[]{:S(2)}) async-start(), calls=%async_computation.22 | async-start | bytes 2621440 | tf_op jit(solution)/shard_map/reduce_scatter | solution.py:401
  703.5 202.7 %reduce-scatter.21.cloned.1.call-start = ((), (), s32[]{:S(2)}) async-start(), calls=%async_computation.24 | async-start | bytes 10485760 | tf_op jit(solution)/shard_map/reduce_scatter | solution.py:401
  725.0 255.6 %reduce-scatter.23.cloned.1.call-start = ((), (), s32[]{:S(2)}) async-start(), calls=%async_computation.25 | async-start | bytes 10485760 | tf_op jit(solution)/shard_map/reduce_scatter | solution.py:401
  750.2 451.9 %all-reduce.14.cloned.1.call-start = ((), (), s32[]{:S(2)}) async-start(), calls=%async_computation.26 | async-start | bytes 12582912 | tf_op jit(solution)/shard_map/psum | solution.py:403
  (114 other events, 1975.2 us)
Sparse Core Ops, SparseCore 0:
  9.6 25.2 all-gather.26
  36.5 22.5 all-gather.22
  60.7 22.6 all-gather.20
  85.9 49.3 all-gather.28
  137.8 47.2 all-gather.24
  187.6 48.3 all-gather.38
  238.7 47.7 all-gather.36
  288.0 21.0 all-gather.30
  310.7 58.2 all-gather.32
  370.5 58.3 all-gather.34
  514.7 88.1 reduce-scatter.8
  607.4 87.8 reduce-scatter.10
  697.8 31.1 reduce-scatter.12
  731.5 31.3 reduce-scatter.18
  765.9 31.4 reduce-scatter.14
  800.5 31.3 reduce-scatter.16
  834.4 71.7 reduce-scatter.20
  908.8 71.7 reduce-scatter.22
  985.5 216.4 all-reduce.13
